TPU v7x, 32 devices: a whole 2x2x4 slice. The times are simulated.
32 devices in a mesh: dp: 4 (over y, x), seq: 8 (over z, core).
Axes of the slice: x: 2, y: 2, z: 4, core: 2. Of those that a mesh axis runs over, the one named last changes fastest.
Arguments:
- hidden_in: bfloat16 [8, 1024, 1536], P('dp', 'seq'), may hold values from -6 to 6
- lengths: int32 [8], P('dp'), may hold values from 256 to 1024, as said below
- cotangent: bfloat16 [8, 1024, 1536], P('dp', 'seq'), may hold values from -6 to 6
- attn_gain: bfloat16 [1536], P(('dp', 'seq')), may hold values from 0.25 to 1.75
- q_weight: bfloat16 [1536, 1536], P(('dp', 'seq')), may hold values from -0.15625 to 0.15625
- q_bias: bfloat16 [1536], P(('dp', 'seq')), may hold values from -3 to 3
- k_weight: bfloat16 [256, 1536], P(('dp', 'seq')), may hold values from -0.15625 to 0.15625
- k_bias: bfloat16 [256], P(('dp', 'seq')), may hold values from -3 to 3
- v_weight: bfloat16 [256, 1536], P(('dp', 'seq')), may hold values from -0.15625 to 0.15625
- v_bias: bfloat16 [256], P(('dp', 'seq')), may hold values from -0.59765625 to 0.59765625
- o_weight: bfloat16 [1536, 1536], P(('dp', 'seq')), may hold values from -0.875 to 0.875
- mlp_gain: bfloat16 [1536], P(('dp', 'seq')), may hold values from 0.25 to 1.75
- gate_weight: bfloat16 [8960, 1536], P(('dp', 'seq')), may hold values from -0.15625 to 0.15625
- up_weight: bfloat16 [8960, 1536], P(('dp', 'seq')), may hold values from -0.15625 to 0.15625
- down_weight: bfloat16 [1536, 8960], P(None, ('dp', 'seq')), may hold values from -0.0625 to 0.0625
Outputs:
- block_out: bfloat16 [8, 1024, 1536], P('dp', 'seq')
- input_grad: float32 [8, 1024, 1536], P('dp', 'seq')
- attn_gain_grad: float32 [1536], P(('dp', 'seq'))
- q_weight_grad: float32 [1536, 1536], P(('dp', 'seq'))
- q_bias_grad: float32 [1536], P(('dp', 'seq'))
- k_weight_grad: float32 [256, 1536], P(('dp', 'seq'))
- k_bias_grad: float32 [256], P(('dp', 'seq'))
- v_weight_grad: float32 [256, 1536], P(('dp', 'seq'))
- v_bias_grad: float32 [256], P(('dp', 'seq'))
- o_weight_grad: float32 [1536, 1536], P(('dp', 'seq'))
- mlp_gain_grad: float32 [1536], P(('dp', 'seq'))
- gate_weight_grad: float32 [8960, 1536], P(('dp', 'seq'))
- up_weight_grad: float32 [8960, 1536], P(('dp', 'seq'))
- down_weight_grad: float32 [1536, 8960], P(None, ('dp', 'seq'))
Inputs may be any that keep to these rules, and one draw needn't show every extreme that they name: Slots t < lengths[b] of sequence b are valid; in every draw at least one sequence is valid in all 1024 slots.
All inputs are finite; a program needn't handle non-finite values.
Results may differ from a plain program's by a relative error of at most 0.025.
Values may be sent and summed in bfloat16 or wider, within the bound.
No kernel may reach another device: no remote copies, remote signals or barrier semaphores. Data moves between devices by JAX's collectives and lax.ppermute only.
A program may use at most 448 MiB of HBM per device.

v0:
```python
import math
import jax
import jax.numpy as jnp
from jax import lax
from jax.sharding import PartitionSpec as P

HEADS = 12
KV_HEADS = 2
HEAD = 128
EPSILON = 1e-06
NEGATIVE = -1e30


def times_transposed(left_side, right_side):
    return lax.dot_general(
        left_side, right_side, (((1,), (1,)), ((), ())), preferred_element_type=jnp.float32
    )


def plain_product(left_side, right_side):
    return jnp.dot(left_side, right_side, preferred_element_type=jnp.float32)


def split_columns(values, group_count):
    row_count, width = values.shape
    return values.reshape(row_count, group_count, width // group_count)


def owner_grad(columns, inputs_all):
    part_grad = jnp.einsum("rpf,rd->pfd", columns, inputs_all, preferred_element_type=jnp.float32)
    return part_grad.reshape(-1, inputs_all.shape[1])


def owner_bias(columns):
    return jnp.sum(columns.astype(jnp.float32), axis=0).reshape(-1)


def rope_tables(positions):
    half_size = HEAD // 2
    inverse = jnp.exp(-math.log(1000000.0) * 2.0 * jnp.arange(half_size).astype(jnp.float32) / HEAD)
    angles = positions[:, None] * inverse[None, :]
    angles = jnp.concatenate([angles, angles], axis=1)
    return (jnp.cos(angles), jnp.sin(angles))


def rotate(values, cosine, sine_table):
    half_size = HEAD // 2
    turned = jnp.concatenate([-values[..., half_size:], values[..., :half_size]], axis=-1)
    return values * cosine[:, None, :] + turned * sine_table[:, None, :]


def rotate_back(gradient, cosine, sine_table):
    half_size = HEAD // 2
    scaled = gradient * sine_table[:, None, :]
    turned = jnp.concatenate([scaled[..., half_size:], -scaled[..., :half_size]], axis=-1)
    return gradient * cosine[:, None, :] + turned


def rms_parts(values):
    inverse = lax.rsqrt(jnp.mean(values * values, axis=-1, keepdims=True) + EPSILON)
    return (values * inverse, inverse)


def rms_back(upstream, normal_values, inverse, gain_values):
    scaled = upstream * gain_values
    gain_grad = jnp.sum(upstream * normal_values, axis=0)
    input_part = inverse * (
        scaled - normal_values * jnp.mean(scaled * normal_values, axis=-1, keepdims=True)
    )
    return (input_part, gain_grad)


def masked_scores(query_heads, key_heads, causal, score_scale):
    scores = (
        jnp.einsum("qkgd,skd->kgqs", query_heads, key_heads, preferred_element_type=jnp.float32)
        * score_scale
    )
    return jnp.where(causal[None, None], scores, NEGATIVE)


def on_device(
    hidden_in,
    lengths,
    cotangent,
    attn_gain,
    q_weight,
    q_bias,
    k_weight,
    k_bias,
    v_weight,
    v_bias,
    o_weight,
    mlp_gain,
    gate_weight,
    up_weight,
    down_weight,
):
    micro_count, span_rows, model_width = hidden_in.shape
    rows = micro_count * span_rows
    full_len = span_rows * lax.axis_size("seq")
    dp_count = lax.axis_size("dp")
    group_share = HEADS // KV_HEADS
    kv_width = KV_HEADS * HEAD
    score_scale = 1.0 / math.sqrt(HEAD)
    positions = lax.axis_index("seq") * span_rows + jnp.arange(span_rows, dtype=jnp.int32)
    cosine, sine_table = rope_tables(positions.astype(jnp.float32))
    causal = positions[:, None] >= jnp.arange(full_len, dtype=jnp.int32)[None, :]
    gathered = (
        lax.all_gather(attn_gain, ("dp", "seq"), axis=0, tiled=True),
        lax.all_gather(q_weight, ("dp", "seq"), axis=0, tiled=True),
        lax.all_gather(q_bias, ("dp", "seq"), axis=0, tiled=True),
        lax.all_gather(k_weight, ("dp", "seq"), axis=0, tiled=True),
        lax.all_gather(k_bias, ("dp", "seq"), axis=0, tiled=True),
        lax.all_gather(v_weight, ("dp", "seq"), axis=0, tiled=True),
        lax.all_gather(v_bias, ("dp", "seq"), axis=0, tiled=True),
        lax.all_gather(o_weight, ("dp", "seq"), axis=0, tiled=True),
        lax.all_gather(mlp_gain, ("dp", "seq"), axis=0, tiled=True),
    )
    gain_one, query_w, query_b, key_w, key_b, value_w, value_b, output_w, gain_two = gathered
    inputs = hidden_in.reshape(rows, model_width).astype(jnp.float32)
    normal_one, inverse_one = rms_parts(inputs)
    attn_in = (normal_one * gain_one.astype(jnp.float32)).astype(jnp.bfloat16)
    query_lin = times_transposed(attn_in, query_w) + query_b.astype(jnp.float32)
    key_lin = times_transposed(attn_in, key_w) + key_b.astype(jnp.float32)
    value_lin = times_transposed(attn_in, value_w) + value_b.astype(jnp.float32)
    query_rot = rotate(
        query_lin.reshape(micro_count, span_rows, HEADS, HEAD), cosine, sine_table
    ).astype(jnp.bfloat16)
    key_rot = (
        rotate(key_lin.reshape(micro_count, span_rows, KV_HEADS, HEAD), cosine, sine_table)
        .astype(jnp.bfloat16)
        .reshape(micro_count, span_rows, kv_width)
    )
    value_low = value_lin.astype(jnp.bfloat16).reshape(micro_count, span_rows, kv_width)
    key_all, value_all = (
        lax.all_gather(key_rot, "seq", axis=1, tiled=True),
        lax.all_gather(value_low, "seq", axis=1, tiled=True),
    )
    query_heads = query_rot.reshape(micro_count, span_rows, KV_HEADS, group_share, HEAD)
    key_heads = key_all.reshape(micro_count, full_len, KV_HEADS, HEAD)
    value_heads = value_all.reshape(micro_count, full_len, KV_HEADS, HEAD)
    mixed_parts = []
    log_parts = []
    for batch_index in range(micro_count):
        scores = masked_scores(
            query_heads[batch_index], key_heads[batch_index], causal, score_scale
        )
        row_top = jnp.max(scores, axis=-1, keepdims=True)
        exponent = jnp.exp(scores - row_top)
        row_total = jnp.sum(exponent, axis=-1, keepdims=True)
        log_parts.append(row_top + jnp.log(row_total))
        soft_low = (exponent / row_total).astype(jnp.bfloat16)
        mixed_heads = jnp.einsum(
            "kgqs,skd->qkgd", soft_low, value_heads[batch_index], preferred_element_type=jnp.float32
        )
        mixed_parts.append(mixed_heads.reshape(span_rows, model_width))
    mixed_low = jnp.concatenate(mixed_parts, axis=0).astype(jnp.bfloat16)
    resid = inputs + times_transposed(mixed_low, output_w)
    normal_two, inverse_two = rms_parts(resid)
    mlp_in = (normal_two * gain_two.astype(jnp.float32)).astype(jnp.bfloat16)
    gate_w, up_w, down_w = (
        lax.all_gather(gate_weight, ("dp", "seq"), axis=0, tiled=True),
        lax.all_gather(up_weight, ("dp", "seq"), axis=0, tiled=True),
        lax.all_gather(down_weight, ("dp", "seq"), axis=1, tiled=True),
    )
    gate_lin = times_transposed(mlp_in, gate_w)
    up_lin = times_transposed(mlp_in, up_w)
    gate_sigma = jax.nn.sigmoid(gate_lin)
    hidden_low = (gate_lin * gate_sigma * up_lin).astype(jnp.bfloat16)
    result = resid + times_transposed(hidden_low, down_w)
    valid_rows = (positions[None, :] < lengths[:, None]).reshape(rows)
    block_out = (
        jnp.where(valid_rows[:, None], result, 0.0)
        .astype(jnp.bfloat16)
        .reshape(micro_count, span_rows, model_width)
    )
    back_query, back_key, back_value, back_output, back_gate, back_up, back_down = (
        lax.all_gather(q_weight, ("dp", "seq"), axis=0, tiled=True),
        lax.all_gather(k_weight, ("dp", "seq"), axis=0, tiled=True),
        lax.all_gather(v_weight, ("dp", "seq"), axis=0, tiled=True),
        lax.all_gather(o_weight, ("dp", "seq"), axis=0, tiled=True),
        lax.all_gather(gate_weight, ("dp", "seq"), axis=0, tiled=True),
        lax.all_gather(up_weight, ("dp", "seq"), axis=0, tiled=True),
        lax.all_gather(down_weight, ("dp", "seq"), axis=1, tiled=True),
    )
    upstream = jnp.where(
        valid_rows[:, None], cotangent.reshape(rows, model_width).astype(jnp.float32), 0.0
    )
    upstream_low = upstream.astype(jnp.bfloat16)
    attn_all, mixed_all, mlp_all, upstream_all = (
        lax.all_gather(attn_in, "seq", axis=0, tiled=True),
        lax.all_gather(mixed_low, "seq", axis=0, tiled=True),
        lax.all_gather(mlp_in, "seq", axis=0, tiled=True),
        lax.all_gather(upstream_low, "seq", axis=0, tiled=True),
    )
    hidden_grad = plain_product(upstream_low, back_down)
    gate_grad = (
        hidden_grad * up_lin * (gate_sigma * (1.0 + gate_lin * (1.0 - gate_sigma)))
    ).astype(jnp.bfloat16)
    up_grad = (hidden_grad * gate_lin * gate_sigma).astype(jnp.bfloat16)
    mlp_in_grad = plain_product(gate_grad, back_gate) + plain_product(up_grad, back_up)
    hidden_cols, gate_cols, up_cols = (
        lax.all_to_all(
            split_columns(hidden_low, dp_count), "seq", split_axis=2, concat_axis=0, tiled=True
        ),
        lax.all_to_all(
            split_columns(gate_grad, dp_count), "seq", split_axis=2, concat_axis=0, tiled=True
        ),
        lax.all_to_all(
            split_columns(up_grad, dp_count), "seq", split_axis=2, concat_axis=0, tiled=True
        ),
    )
    down_grad = jnp.einsum(
        "rd,rpf->dpf", upstream_all, hidden_cols, preferred_element_type=jnp.float32
    ).reshape(model_width, -1)
    gate_w_grad = owner_grad(gate_cols, mlp_all)
    up_w_grad = owner_grad(up_cols, mlp_all)
    norm_two_grad, gain_two_grad = rms_back(
        mlp_in_grad, normal_two, inverse_two, gain_two.astype(jnp.float32)
    )
    resid_grad = upstream + norm_two_grad
    resid_low = resid_grad.astype(jnp.bfloat16)
    mixed_grad = (
        plain_product(resid_low, back_output)
        .astype(jnp.bfloat16)
        .reshape(micro_count, span_rows, KV_HEADS, group_share, HEAD)
    )
    query_parts = []
    key_parts = []
    value_parts = []
    for batch_index in range(micro_count):
        again_scores = masked_scores(
            query_heads[batch_index], key_heads[batch_index], causal, score_scale
        )
        soft_probs = jnp.exp(again_scores - log_parts[batch_index])
        probs_low = soft_probs.astype(jnp.bfloat16)
        prob_grad = jnp.einsum(
            "qkgd,skd->kgqs",
            mixed_grad[batch_index],
            value_heads[batch_index],
            preferred_element_type=jnp.float32,
        )
        value_all_grad = jnp.einsum(
            "kgqs,qkgd->skd", probs_low, mixed_grad[batch_index], preferred_element_type=jnp.float32
        )
        row_delta = jnp.sum(soft_probs * prob_grad, axis=-1, keepdims=True)
        score_grad = (soft_probs * (prob_grad - row_delta)).astype(jnp.bfloat16)
        query_parts.append(
            jnp.einsum(
                "kgqs,skd->qkgd",
                score_grad,
                key_heads[batch_index],
                preferred_element_type=jnp.float32,
            )
            * score_scale
        )
        key_parts.append(
            (
                jnp.einsum(
                    "kgqs,qkgd->skd",
                    score_grad,
                    query_heads[batch_index],
                    preferred_element_type=jnp.float32,
                )
                * score_scale
            ).reshape(full_len, kv_width)
        )
        value_parts.append(value_all_grad.reshape(full_len, kv_width))
    key_grad, value_grad = (
        lax.psum_scatter(jnp.stack(key_parts), "seq", scatter_dimension=1, tiled=True),
        lax.psum_scatter(jnp.stack(value_parts), "seq", scatter_dimension=1, tiled=True),
    )
    query_grad = jnp.stack(query_parts).reshape(micro_count, span_rows, HEADS, HEAD)
    query_low = (
        rotate_back(query_grad, cosine, sine_table).reshape(rows, model_width).astype(jnp.bfloat16)
    )
    key_low = (
        rotate_back(key_grad.reshape(micro_count, span_rows, KV_HEADS, HEAD), cosine, sine_table)
        .reshape(rows, kv_width)
        .astype(jnp.bfloat16)
    )
    value_grad_low = value_grad.reshape(rows, kv_width).astype(jnp.bfloat16)
    attn_in_grad = (
        plain_product(query_low, back_query)
        + plain_product(key_low, back_key)
        + plain_product(value_grad_low, back_value)
    )
    norm_one_grad, gain_one_grad = rms_back(
        attn_in_grad, normal_one, inverse_one, gain_one.astype(jnp.float32)
    )
    input_grad = (resid_grad + norm_one_grad).reshape(micro_count, span_rows, model_width)
    resid_cols, query_cols, key_cols, value_cols = (
        lax.all_to_all(
            split_columns(resid_low, dp_count), "seq", split_axis=2, concat_axis=0, tiled=True
        ),
        lax.all_to_all(
            split_columns(query_low, dp_count), "seq", split_axis=2, concat_axis=0, tiled=True
        ),
        lax.all_to_all(
            split_columns(key_low, dp_count), "seq", split_axis=2, concat_axis=0, tiled=True
        ),
        lax.all_to_all(
            split_columns(value_grad_low, dp_count), "seq", split_axis=2, concat_axis=0, tiled=True
        ),
    )
    output_w_grad = owner_grad(resid_cols, mixed_all)
    query_w_grad = owner_grad(query_cols, attn_all)
    key_w_grad = owner_grad(key_cols, attn_all)
    value_w_grad = owner_grad(value_cols, attn_all)
    query_b_grad = owner_bias(query_cols)
    key_b_grad = owner_bias(key_cols)
    value_b_grad = owner_bias(value_cols)
    totals = (
        lax.psum_scatter(
            query_w_grad.astype(jnp.bfloat16), "dp", scatter_dimension=0, tiled=True
        ).astype(jnp.float32),
        lax.psum_scatter(
            query_b_grad.astype(jnp.bfloat16), "dp", scatter_dimension=0, tiled=True
        ).astype(jnp.float32),
        lax.psum_scatter(
            key_w_grad.astype(jnp.bfloat16), "dp", scatter_dimension=0, tiled=True
        ).astype(jnp.float32),
        lax.psum_scatter(
            key_b_grad.astype(jnp.bfloat16), "dp", scatter_dimension=0, tiled=True
        ).astype(jnp.float32),
        lax.psum_scatter(
            value_w_grad.astype(jnp.bfloat16), "dp", scatter_dimension=0, tiled=True
        ).astype(jnp.float32),
        lax.psum_scatter(
            value_b_grad.astype(jnp.bfloat16), "dp", scatter_dimension=0, tiled=True
        ).astype(jnp.float32),
        lax.psum_scatter(
            output_w_grad.astype(jnp.bfloat16), "dp", scatter_dimension=0, tiled=True
        ).astype(jnp.float32),
        lax.psum_scatter(
            gate_w_grad.astype(jnp.bfloat16), "dp", scatter_dimension=0, tiled=True
        ).astype(jnp.float32),
        lax.psum_scatter(
            up_w_grad.astype(jnp.bfloat16), "dp", scatter_dimension=0, tiled=True
        ).astype(jnp.float32),
        lax.psum_scatter(
            down_grad.astype(jnp.bfloat16), "dp", scatter_dimension=1, tiled=True
        ).astype(jnp.float32),
    )
    gain_totals = (
        lax.psum_scatter(gain_one_grad, ("dp", "seq"), scatter_dimension=0, tiled=True),
        lax.psum_scatter(gain_two_grad, ("dp", "seq"), scatter_dimension=0, tiled=True),
    )
    return (
        block_out,
        input_grad,
        gain_totals[0],
        totals[0],
        totals[1],
        totals[2],
        totals[3],
        totals[4],
        totals[5],
        totals[6],
        gain_totals[1],
        totals[7],
        totals[8],
        totals[9],
    )


def solution(mesh):
    placed = (
        P("dp", "seq", None),
        P("dp"),
        P("dp", "seq", None),
        P(("dp", "seq")),
        P(("dp", "seq"), None),
        P(("dp", "seq")),
        P(("dp", "seq"), None),
        P(("dp", "seq")),
        P(("dp", "seq"), None),
        P(("dp", "seq")),
        P(("dp", "seq"), None),
        P(("dp", "seq")),
        P(("dp", "seq"), None),
        P(("dp", "seq"), None),
        P(None, ("dp", "seq")),
    )
    return jax.shard_map(
        on_device,
        mesh=mesh,
        in_specs=placed,
        out_specs=(
            P("dp", "seq", None),
            P("dp", "seq", None),
            P(("dp", "seq")),
            P(("dp", "seq"), None),
            P(("dp", "seq")),
            P(("dp", "seq"), None),
            P(("dp", "seq")),
            P(("dp", "seq"), None),
            P(("dp", "seq")),
            P(("dp", "seq"), None),
            P(("dp", "seq")),
            P(("dp", "seq"), None),
            P(("dp", "seq"), None),
            P(None, ("dp", "seq")),
        ),
        check_vma=False,
    )
```

profile of v0, /device:TPU:0, one launch (start us, length us, event | category | flops | bytes accessed | tf_op | source)
XLA Modules:
  0.0 1691.5 jit_solution(5494307519598988704)
XLA Ops:
  11.5 42.2 %all-reduce.16 = (bf16[1536]{0:T(1024)(128)(2,1)S(1)}, bf16[256]{0:T(256)(128)(2,1)S(1)}, bf16[256]{0:T(256)(128)(2,1)S(1)}, bf16[1536]{0:T(1024)(128)(2,1)S(1)}, bf16[1536]{0:T(1024)(128)(2,1)S(1)}) all-reduce(bf16[1536]{0:T(1024)(128)(2,1)S(1)} %dynamic-update-slice, ...), channel_id=1, replica_groups=mesh['dp'=4,'seq'=8] {'dp','seq'}, use_global_device_ids=true, to_apply=%add | all-reduce | flops 5120 | bytes 20480
  55.1 43.7 %all_gather.62 = bf16[256,1536]{1,0:T(8,128)(2,1)S(1)} all-gather(bf16[8,1536]{1,0:T(8,128)(2,1)} %param.23), channel_id=1, replica_groups=mesh['dp'=4,'seq'=8] {'dp','seq'}, dimensions={0}, use_global_device_ids=true | all-gather | bytes 811008 | tf_op jit(solution)/shard_map/all_gather | solution.py:114
  101.7 41.4 %all_gather.65 = bf16[256,1536]{1,0:T(8,128)(2,1)S(1)} all-gather(bf16[8,1536]{1,0:T(8,128)(2,1)S(1)} %copy-done.51), channel_id=1, replica_groups=mesh['dp'=4,'seq'=8] {'dp','seq'}, dimensions={0}, use_global_device_ids=true | all-gather | bytes 811008 | tf_op jit(solution)/shard_map/all_gather | solution.py:112
  155.0 13.8 all-gather.14.cloned.1.call-done
  171.2 63.2 %all-gather.16.cloned.1.call-done = bf16[1536,1536]{1,0:T(8,128)(2,1)} async-done(((bf16[48,1536]{1,0:T(8,128)(2,1)}), bf16[1536,1536]{1,0:T(8,128)(2,1)}) %all-gather.16.cloned.1.call-update) | async-done | bytes 4718608 | tf_op jit(solution)/shard_map/all_gather | solution.py:110
  234.3 4.9 convolution_add_fusion.5
  257.0 42.2 %all-gather.18.cloned.1.call-done = bf16[1536,1536]{1,0:T(8,128)(2,1)} async-done(((bf16[48,1536]{1,0:T(8,128)(2,1)}), bf16[1536,1536]{1,0:T(8,128)(2,1)}) %all-gather.18.cloned.1.call-update) | async-done | bytes 4718608 | tf_op jit(solution)/shard_map/all_gather | solution.py:116
  299.2 3.9 multiply_reduce_fusion.4
  303.9 161.8 %all-gather.20.cloned.1.call-done = bf16[8960,1536]{1,0:T(8,128)(2,1)} async-done(((bf16[280,1536]{1,0:T(8,128)(2,1)}), bf16[8960,1536]{1,0:T(8,128)(2,1)}) %all-gather.20.cloned.1.call-update) | async-done | bytes 27525136 | tf_op jit(solution)/shard_map/all_gather | solution.py:162
  465.8 16.7 fusion.50
  482.5 149.7 %all-gather.22.cloned.1.call-done = bf16[8960,1536]{1,0:T(8,128)(2,1)} async-done(((bf16[280,1536]{1,0:T(8,128)(2,1)}), bf16[8960,1536]{1,0:T(8,128)(2,1)}) %all-gather.22.cloned.1.call-update) | async-done | bytes 27525136 | tf_op jit(solution)/shard_map/all_gather | solution.py:163
  632.2 16.4 fusion.51
  648.7 150.2 %all-gather.24.cloned.1.call-done = bf16[1536,8960]{0,1:T(8,128)(2,1)} async-done(((bf16[1536,280]{0,1:T(8,128)(2,1)}), bf16[1536,8960]{0,1:T(8,128)(2,1)}) %all-gather.24.cloned.1.call-update) | async-done | bytes 27525136 | tf_op jit(solution)/shard_map/all_gather | solution.py:164
  798.9 20.1 %multiply_convert_fusion = (bf16[256,8960]{1,0:T(8,128)(2,1)S(1)}, bf16[256,8960]{1,0:T(8,128)(2,1)}, bf16[256,8960]{1,0:T(8,128)(2,1)}) fusion(f32[256,8960]{1,0:T(8,128)} %fusion.50, f32[256,8960]{1,0:T(8,128)} %fusion.51, bf16[256,1536]{1,0:T(8,128)(2,1)S(1)} %copy-done.24, bf16[1536,8960]{0,1:T(8,128)(2,1)} %all-gather.24.cloned.1.call-done), kind=kOutput, calls=%fused_computation | convolution fusion | flops 7083130880 | bytes 60424192 | tf_op jit(solution)/shard_map/dot_general | solution.py:21
  819.0 16.4 fusion.52
  835.5 14.8 multiply_reduce_fusion
  854.5 4.4 fusion.3
  867.5 4.5 fusion
  878.1 4.0 fusion.12
  882.5 4.0 fusion.10
  892.6 2.6 reshape.329
  897.7 4.2 all-to-all-start.3
  910.6 14.6 all-to-all-done.3
  925.2 3.5 all-to-all-start
  931.8 28.9 %all-to-all-done = bf16[256,4,384]{0,1,2:T(4,128)(2,1)S(1)} async-done(((bf16[256,4,384]{0,1,2:T(4,128)(2,1)}), bf16[256,4,384]{0,1,2:T(4,128)(2,1)S(1)}, u32[]{:S(2)}, u32[]{:S(2)}) %all-to-all-start) | async-done | bytes 786464 | tf_op jit(solution)/shard_map/all_to_all | solution.py:296
  960.7 4.1 all-to-all-start.1
  966.8 4.8 all-to-all-done.1
  971.5 3.6 all-to-all-start.2
  975.1 6.7 copy.145
  981.9 18.3 %copy.146 = bf16[256,4,2240]{0,1,2:T(4,128)(2,1)} copy(bf16[256,4,2240]{0,2,1:T(8,128)(2,1)} %bitcast.310) | data formatting | bytes 9175040 | tf_op jit(solution)/shard_map/reshape | solution.py:26
  1000.2 5.1 all-to-all-start.4
  1006.6 57.7 %all-gather.28.cloned.1.call-done = bf16[2048,1536]{0,1:T(8,128)(2,1)} async-done(((bf16[256,1536]{0,1:T(8,128)(2,1)}), bf16[2048,1536]{0,1:T(8,128)(2,1)}) %all-gather.28.cloned.1.call-update) | async-done | bytes 6291472 | tf_op jit(solution)/shard_map/all_gather | solution.py:192
  1064.3 5.9 convolution_convert_fusion.4
  1070.2 6.5 copy.149
  1076.7 18.2 %copy.150 = bf16[256,4,2240]{0,1,2:T(4,128)(2,1)} copy(bf16[256,4,2240]{0,2,1:T(8,128)(2,1)} %bitcast.311) | data formatting | bytes 9175040 | tf_op jit(solution)/shard_map/reshape | solution.py:26
  1094.9 83.9 %all-to-all-done.4 = bf16[256,4,2240]{0,1,2:T(4,128)(2,1)} async-done(((bf16[256,4,2240]{0,1,2:T(4,128)(2,1)}), bf16[256,4,2240]{0,1,2:T(4,128)(2,1)}, u32[]{:S(2)}, u32[]{:S(2)}) %all-to-all-start.4) | async-done | bytes 4587552 | tf_op jit(solution)/shard_map/all_to_all | solution.py:206
  1178.8 5.3 all-to-all-start.5
  1184.4 5.0 convolution_convert_fusion.5
  1190.0 5.3 convolution_convert_fusion.7
  1197.1 2.9 copy.147
  1200.0 2.7 copy.200
  1202.7 115.3 %all-gather.30.cloned.1.call-done = bf16[2048,1536]{1,0:T(8,128)(2,1)} async-done(((bf16[256,1536]{1,0:T(8,128)(2,1)}), bf16[2048,1536]{1,0:T(8,128)(2,1)}) %all-gather.30.cloned.1.call-update) | async-done | bytes 6291472 | tf_op jit(solution)/shard_map/all_gather | solution.py:193
  1318.0 12.0 convolution_convert_fusion.2
  1330.0 6.6 copy.153
  1336.6 18.2 %copy.154 = bf16[256,4,2240]{0,1,2:T(4,128)(2,1)} copy(bf16[256,4,2240]{0,2,1:T(8,128)(2,1)} %bitcast.315) | data formatting | bytes 9175040 | tf_op jit(solution)/shard_map/reshape | solution.py:26
  1354.8 4.8 all-to-all-done.5
  1359.6 4.6 all-to-all-start.6
  1364.3 3.1 copy.151
  1369.2 8.7 convolution_convert_fusion.1
  1378.2 108.3 %all-to-all-done.6 = bf16[256,4,2240]{0,1,2:T(4,128)(2,1)} async-done(((bf16[256,4,2240]{0,1,2:T(4,128)(2,1)}), bf16[256,4,2240]{0,1,2:T(4,128)(2,1)}, u32[]{:S(2)}, u32[]{:S(2)}) %all-to-all-start.6) | async-done | bytes 4587552 | tf_op jit(solution)/shard_map/all_to_all | solution.py:203
  1486.4 2.9 copy.155
  1489.4 2.7 copy.202
  1492.1 12.0 convolution_convert_fusion
  1507.0 5.0 fusion.30
  1512.0 14.4 fusion.19
  1533.6 3.1 multiply_reduce_fusion.1
  1536.7 37.7 %all-reduce.15 = (f32[1536]{0:T(1024)S(1)}, f32[1536]{0:T(1024)S(1)}) all-reduce(f32[1536]{0:T(1024)S(1)} %get-tuple-element.16, f32[1536]{0:T(1024)} %get-tuple-element.14), channel_id=4, replica_groups=mesh['dp'=4,'seq'=8] {'dp','seq'}, use_global_device_ids=true, to_apply=%region_13.14.clone | all-reduce | flops 3072 | bytes 24576
  1576.3 3.0 multiply_add_fusion
  1579.7 10.5 all-reduce.17
  1592.8 2.6 convert_element_type.250
  1595.4 37.4 %reduce-scatter.24.cloned.1.call-done = bf16[280,1536]{1,0:T(8,128)(2,1)} async-done(((bf16[1120,1536]{1,0:T(8,128)(2,1)}), bf16[280,1536]{1,0:T(8,128)(2,1)}) %reduce-scatter.24.cloned.1.call-update) | async-done | bytes 860176
  1632.7 2.6 convert_element_type.252
  1635.3 46.9 %reduce-scatter.26.cloned.1.call-done = bf16[1536,280]{0,1:T(8,128)(2,1)} async-done(((bf16[1536,1120]{0,1:T(8,128)(2,1)}), bf16[1536,280]{0,1:T(8,128)(2,1)}) %reduce-scatter.26.cloned.1.call-update) | async-done | bytes 860176
  1682.2 2.6 convert_element_type.254
  (319 shorter events, 101.3 us)
Async XLA Ops:
  7.2 94.5 %copy-start.51 = (bf16[8,1536]{1,0:T(8,128)(2,1)S(1)}, bf16[8,1536]{1,0:T(8,128)(2,1)}, u32[]{:S(2)}) copy-start(bf16[8,1536]{1,0:T(8,128)(2,1)} %param.21) | copy-start | bytes 73732
  7.2 144.6 %all-gather.12.cloned.1.call-start = ((), (), s32[]{:S(2)}) async-start(), calls=%async_computation.14 | async-start | bytes 1179648 | tf_op jit(solution)/shard_map/all_gather | solution.py:137
  53.7 45.1 %copy-start.41 = (f32[1536]{0:T(1024)}, f32[1536]{0:T(1024)S(1)}, u32[]{:S(2)}) copy-start(f32[1536]{0:T(1024)S(1)} %convert_element_type.200) | copy-start | bytes 18436
  55.1 43.7 %copy-start.52 = (f32[256]{0:T(256)}, f32[256]{0:T(256)S(1)}, u32[]{:S(2)}) copy-start(f32[256]{0:T(256)S(1)} %rsqrt_bitcast_fusion) | copy-start | bytes 3076
  100.5 133.8 %copy-start.9 = (bf16[256,1536]{1,0:T(8,128)(2,1)}, bf16[256,1536]{1,0:T(8,128)(2,1)S(1)}, u32[]{:S(2)}) copy-start(bf16[256,1536]{1,0:T(8,128)(2,1)S(1)} %multiply_convert_fusion.4) | copy-start | bytes 2359300
  101.6 67.3 %all-gather.14.cloned.1.call-start = ((), (), s32[]{:S(2)}) async-start(), calls=%async_computation.15 | async-start | bytes 1179648 | tf_op jit(solution)/shard_map/all_gather | solution.py:136
  143.9 6.5 copy-start.58
  143.9 6.7 copy-start.21
  145.8 96.7 %copy-start.30 = (f32[128,128]{0,1:T(8,128)}, f32[128,128]{0,1:T(8,128)S(1)}, u32[]{:S(2)}) copy-start(f32[128,128]{0,1:T(8,128)S(1)} %get-tuple-element.51) | copy-start | bytes 196612
  145.8 96.7 %copy-start.32 = (f32[128,128]{0,1:T(8,128)}, f32[128,128]{0,1:T(8,128)S(1)}, u32[]{:S(2)}) copy-start(f32[128,128]{0,1:T(8,128)S(1)} %get-tuple-element.52) | copy-start | bytes 196612
  146.6 87.8 %all-gather.16.cloned.1.call-start = ((), (), s32[]{:S(2)}) async-start(), calls=%async_computation.16 | async-start | bytes 4866048 | tf_op jit(solution)/shard_map/all_gather | solution.py:110
  147.3 151.8 %all-gather.18.cloned.1.call-start = ((), (), s32[]{:S(2)}) async-start(), calls=%async_computation.17 | async-start | bytes 4866048 | tf_op jit(solution)/shard_map/all_gather | solution.py:116
  147.9 317.9 %all-gather.20.cloned.1.call-start = ((), (), s32[]{:S(2)}) async-start(), calls=%async_computation.18 | async-start | bytes 28385280 | tf_op jit(solution)/shard_map/all_gather | solution.py:162
  148.5 483.8 %all-gather.22.cloned.1.call-start = ((), (), s32[]{:S(2)}) async-start(), calls=%async_computation.19 | async-start | bytes 28385280 | tf_op jit(solution)/shard_map/all_gather | solution.py:163
  149.0 649.8 %all-gather.24.cloned.1.call-start = ((), (), s32[]{:S(2)}) async-start(), calls=%async_computation.20 | async-start | bytes 28385280 | tf_op jit(solution)/shard_map/all_gather | solution.py:164
  149.8 779.3 %reduce-scatter.14.cloned.1.call-start = ((), (), s32[]{:S(2)}) async-start(), calls=%async_computation.21 | async-start | bytes 2359296 | tf_op jit(solution)/shard_map/reduce_scatter | solution.py:270
  242.5 6.6 copy-start.16
  255.5 43.6 %copy-start.38 = (bf16[2,128,6,128]{3,1,2,0:T(8,128)(2,1)}, bf16[2,128,6,128]{3,1,2,0:T(8,128)(2,1)S(1)}, u32[]{:S(2)}) copy-start(bf16[2,128,6,128]{3,1,2,0:T(8,128)(2,1)S(1)} %fusion.28) | copy-start | bytes 1179652
  255.7 43.5 %copy-start.7 = (bf16[2,128,1536]{2,1,0:T(8,128)(2,1)S(1)}, bf16[2,128,1536]{2,1,0:T(8,128)(2,1)}, u32[]{:S(2)}) copy-start(bf16[2,128,1536]{2,1,0:T(8,128)(2,1)} %param.15) | copy-start | bytes 2359300
  256.9 46.2 %copy-start.40 = (bf16[2,128,6,128]{3,1,2,0:T(8,128)(2,1)}, bf16[2,128,6,128]{3,1,2,0:T(8,128)(2,1)S(1)}, u32[]{:S(2)}) copy-start(bf16[2,128,6,128]{3,1,2,0:T(8,128)(2,1)S(1)} %fusion.27) | copy-start | bytes 1179652
  303.1 547.2 %copy-start.13 = (f32[256,1536]{1,0:T(8,128)}, f32[256,1536]{1,0:T(8,128)S(1)}, u32[]{:S(2)}) copy-start(f32[256,1536]{1,0:T(8,128)S(1)} %get-tuple-element.58) | copy-start | bytes 4718596
  303.9 328.3 %copy-start.25 = (bf16[256,1536]{1,0:T(8,128)(2,1)}, bf16[256,1536]{1,0:T(8,128)(2,1)S(1)}, u32[]{:S(2)}) copy-start(bf16[256,1536]{1,0:T(8,128)(2,1)S(1)} %multiply_convert_fusion.3) | copy-start | bytes 2359300
  482.5 316.4 %copy-start.24 = (bf16[256,1536]{1,0:T(8,128)(2,1)S(1)}, bf16[256,1536]{1,0:T(8,128)(2,1)}, u32[]{:S(2)}) copy-start(bf16[256,1536]{1,0:T(8,128)(2,1)} %fusion.24) | copy-start | bytes 2359300
  819.0 16.4 copy-start.17
  819.0 16.4 copy-start.44
  819.0 16.4 copy-start.54
  835.4 16.6 slice-start.8
  835.4 14.9 copy-start.22
  835.4 14.9 copy-start.56
  835.5 16.6 slice-start.9
  852.0 6.9 slice-start
  861.9 10.2 slice-start.2
  878.0 86.8 %reduce-scatter.16.cloned.1.call-start = ((), (), s32[]{:S(2)}) async-start(), calls=%async_computation.22 | async-start | bytes 2359296 | tf_op jit(solution)/shard_map/reduce_scatter | solution.py:271
  888.3 13.6 copy-start.3
  888.3 176.0 %all-gather.28.cloned.1.call-start = ((), (), s32[]{:S(2)}) async-start(), calls=%async_computation.25 | async-start | bytes 7077888 | tf_op jit(solution)/shard_map/all_gather | solution.py:192
  890.5 293.8 %all-gather.26.cloned.1.call-start = ((), (), s32[]{:S(2)}) async-start(), calls=%async_computation.23 | async-start | bytes 7077888 | tf_op jit(solution)/shard_map/all_gather | solution.py:191
  891.3 426.8 %all-gather.30.cloned.1.call-start = ((), (), s32[]{:S(2)}) async-start(), calls=%async_computation.27 | async-start | bytes 7077888 | tf_op jit(solution)/shard_map/all_gather | solution.py:193
  891.9 600.3 %all-gather.32.cloned.1.call-start = ((), (), s32[]{:S(2)}) async-start(), calls=%async_computation.28 | async-start | bytes 7077888 | tf_op jit(solution)/shard_map/all_gather | solution.py:194
  897.7 27.5 %all-to-all-start.3 = ((bf16[256,4,384]{0,1,2:T(4,128)(2,1)}), bf16[256,4,384]{0,1,2:T(4,128)(2,1)}, u32[]{:S(2)}, u32[]{:S(2)}) async-start(bf16[256,4,384]{0,1,2:T(4,128)(2,1)} %copy.142), calls=%async_computation.6 | async-start | bytes 1572864 | tf_op jit(solution)/shard_map/all_to_all | solution.py:293
  925.2 35.5 %all-to-all-start = ((bf16[256,4,384]{0,1,2:T(4,128)(2,1)}), bf16[256,4,384]{0,1,2:T(4,128)(2,1)S(1)}, u32[]{:S(2)}, u32[]{:S(2)}) async-start(bf16[256,4,384]{0,1,2:T(4,128)(2,1)} %copy.133), calls=%async_computation.2 | async-start | bytes 1572864 | tf_op jit(solution)/shard_map/all_to_all | solution.py:296
  960.7 10.9 all-to-all-start.1
  971.5 218.4 %copy-start.34 = (bf16[256,4,64]{0,1,2:T(4,128)(2,1)}, bf16[256,4,64]{0,1,2:T(4,128)(2,1)S(1)}, u32[]{:S(2)}) copy-start(bf16[256,4,64]{0,1,2:T(4,128)(2,1)S(1)} %all-to-all-done.1) | copy-start | bytes 393220
  971.5 28.6 %all-to-all-start.2 = ((bf16[256,4,64]{0,1,2:T(4,128)(2,1)}), bf16[256,4,64]{0,1,2:T(4,128)(2,1)S(1)}, u32[]{:S(2)}, u32[]{:S(2)}) async-start(bf16[256,4,64]{0,1,2:T(4,128)(2,1)} %copy.140), calls=%async_computation.5 | async-start | bytes 262144 | tf_op jit(solution)/shard_map/all_to_all | solution.py:302
  1000.2 189.8 %copy-start.36 = (bf16[256,4,64]{0,1,2:T(4,128)(2,1)}, bf16[256,4,64]{0,1,2:T(4,128)(2,1)S(1)}, u32[]{:S(2)}) copy-start(bf16[256,4,64]{0,1,2:T(4,128)(2,1)S(1)} %all-to-all-done.2) | copy-start | bytes 393220
  1000.2 178.6 %all-to-all-start.4 = ((bf16[256,4,2240]{0,1,2:T(4,128)(2,1)}), bf16[256,4,2240]{0,1,2:T(4,128)(2,1)}, u32[]{:S(2)}, u32[]{:S(2)}) async-start(bf16[256,4,2240]{0,1,2:T(4,128)(2,1)} %copy.146), calls=%async_computation.8 | async-start | bytes 9175040 | tf_op jit(solution)/shard_map/all_to_all | solution.py:206
  1005.2 522.0 %reduce-scatter.20.cloned.1.call-start = ((), (), s32[]{:S(2)}) async-start(), calls=%async_computation.26 | async-start | bytes 737280 | tf_op jit(solution)/shard_map/reduce_scatter | solution.py:332
  1178.8 180.8 %all-to-all-start.5 = ((bf16[256,4,2240]{0,1,2:T(4,128)(2,1)}), bf16[256,4,2240]{0,1,2:T(4,128)(2,1)}, u32[]{:S(2)}, u32[]{:S(2)}) async-start(bf16[256,4,2240]{0,1,2:T(4,128)(2,1)} %copy.150), calls=%async_computation.9 | async-start | bytes 9175040 | tf_op jit(solution)/shard_map/all_to_all | solution.py:209
  1184.1 344.8 %reduce-scatter.18.cloned.1.call-start = ((), (), s32[]{:S(2)}) async-start(), calls=%async_computation.24 | async-start | bytes 737280 | tf_op jit(solution)/shard_map/reduce_scatter | solution.py:314
  1189.4 402.0 %all-reduce.21.cloned.1.call-start = ((), (), s32[]{:S(2)}) async-start(), calls=%async_computation.32 | async-start | bytes 393216
  1197.1 395.7 %reduce-scatter.22.cloned.1.call-start = ((), (), s32[]{:S(2)}) async-start(), calls=%async_computation.29 | async-start | bytes 4300800
  1359.6 126.8 %all-to-all-start.6 = ((bf16[256,4,2240]{0,1,2:T(4,128)(2,1)}), bf16[256,4,2240]{0,1,2:T(4,128)(2,1)}, u32[]{:S(2)}, u32[]{:S(2)}) async-start(bf16[256,4,2240]{0,1,2:T(4,128)(2,1)} %copy.154), calls=%async_computation.10 | async-start | bytes 9175040 | tf_op jit(solution)/shard_map/all_to_all | solution.py:203
  1364.3 268.5 %reduce-scatter.24.cloned.1.call-start = ((), (), s32[]{:S(2)}) async-start(), calls=%async_computation.30 | async-start | bytes 4300800
  1378.0 304.2 %reduce-scatter.26.cloned.1.call-start = ((), (), s32[]{:S(2)}) async-start(), calls=%async_computation.31 | async-start | bytes 4300800
  1492.1 12.1 copy-start.59
  1506.1 5.9 slice-start.4
  1506.1 5.9 copy-start.57
  1512.0 19.8 %copy-start.11 = (bf16[256,1536]{1,0:T(8,128)(2,1)S(1)}, bf16[256,1536]{1,0:T(8,128)(2,1)}, u32[]{:S(2)}) copy-start(bf16[256,1536]{1,0:T(8,128)(2,1)} %copy-done.10) | copy-start | bytes 2359300
  1526.5 7.1 copy-start.8
  1526.5 7.1 copy-start.27
  1526.5 7.2 copy-start.42
  1533.6 42.7 %copy-start.12 = (f32[256,1536]{1,0:T(8,128)S(1)}, f32[256,1536]{1,0:T(8,128)}, u32[]{:S(2)}) copy-start(f32[256,1536]{1,0:T(8,128)} %get-tuple-element.31) | copy-start | bytes 4718596
  1533.6 45.7 %copy-start.35 = (bf16[256,4,64]{0,1,2:T(4,128)(2,1)S(1)}, bf16[256,4,64]{0,1,2:T(4,128)(2,1)}, u32[]{:S(2)}) copy-start(bf16[256,4,64]{0,1,2:T(4,128)(2,1)} %copy-done.34) | copy-start | bytes 393220
  1533.6 45.9 %copy-start.37 = (bf16[256,4,64]{0,1,2:T(4,128)(2,1)S(1)}, bf16[256,4,64]{0,1,2:T(4,128)(2,1)}, u32[]{:S(2)}) copy-start(bf16[256,4,64]{0,1,2:T(4,128)(2,1)} %copy-done.36) | copy-start | bytes 393220
  1536.7 43.0 %copy-start.60 = (bf16[192]{0:T(256)(128)(2,1)S(1)}, bf16[192]{0:T(256)(128)(2,1)}, u32[]{:S(2)}) copy-start(bf16[192]{0:T(256)(128)(2,1)} %convert_element_type.235) | copy-start | bytes 1156
  (33 other events, 90.9 us)
Sparse Core Ops, SparseCore 0:
  101.7 21.0 all-gather.11
  146.7 22.1 all-gather.13
  171.9 62.3 all-gather.15
  237.2 61.8 all-gather.17
  302.0 163.6 all-gather.19
  468.6 163.5 all-gather.21
  635.3 163.5 all-gather.23
  878.1 36.5 reduce-scatter.13
  917.1 45.6 reduce-scatter.15
  964.2 100.0 all-gather.27
  1065.9 117.1 all-gather.25
  1184.7 133.3 all-gather.29
  1320.2 101.5 all-gather.31
  1424.5 35.5 reduce-scatter.19
  1462.8 25.4 reduce-scatter.17
  1491.1 42.6 all-reduce.20
  1536.6 46.9 reduce-scatter.21
  1586.5 46.1 reduce-scatter.23
  1635.8 46.3 reduce-scatter.25
where the time goes:
time: 1700 us; the launch traced here: 1690 us
  waiting for transfers between devices  1090 us (64%)
  matrix products  199 us (12%)
  blocking collectives  176 us (10%)
  local copies, waits for them, and re-layouts  137 us (8%)
  other arithmetic  43.6 us (3%)
  starting transfers between devices  31.8 us (2%)
    all_gather x1, waiting for transfers between devices, on_device(): lax.all_gather(gate_weight, ('dp', 'seq'), axis=0, tiled=True)  162 us
    all_gather x1, waiting for transfers between devices, on_device(): lax.all_gather(down_weight, ('dp', 'seq'), axis=1, tiled=True)  150 us
    all_gather x1, waiting for transfers between devices, on_device(): lax.all_gather(up_weight, ('dp', 'seq'), axis=0, tiled=True)  150 us
    all_gather x1, waiting for transfers between devices, on_device(): lax.all_gather(mlp_in, 'seq', axis=0, tiled=True)  115 us
    all_to_all x1, waiting for transfers between devices, on_device(): lax.all_to_all(split_columns(hidden_low, dp_count), 'seq', split_axis=2,...  108 us
    unnamed x3, blocking collectives  90.4 us
    unnamed x23, waiting for transfers between devices  89.3 us
    all_to_all x1, waiting for transfers between devices, on_device(): lax.all_to_all(split_columns(gate_grad, dp_count), 'seq', split_axis=2, c...  83.9 us
  transfers between devices with their start and end apart: 26, of which 16 were waited for; matrix products, arithmetic and copies ran while one was open for 17% of the time, Pallas kernels for 0%

commit v1 on v0

--- a/solution.py
+++ b/solution.py
@@ -9,6 +9,12 @@
 HEAD = 128
 EPSILON = 1e-06
 NEGATIVE = -1e30
+
+
+def roots_open(local_block, dimension_no):
+    t1 = list(local_block.shape[1:])
+    t1[dimension_no] *= local_block.shape[0]
+    return jnp.moveaxis(local_block, 0, dimension_no).reshape(t1)
 
 
 def times_transposed(left_side, right_side):
@@ -187,9 +193,26 @@
         valid_rows[:, None], cotangent.reshape(rows, model_width).astype(jnp.float32), 0.0
     )
     upstream_low = upstream.astype(jnp.bfloat16)
+
+    def _place_boxes(my_tile, across, dim_i):
+        n_dev_all = lax.axis_size(across)
+        arrivals = list(map(lambda h: (h, (h + 1) % n_dev_all), range(n_dev_all)))
+        blocks_here = [(j, dev_j) for dev_j, j in arrivals]
+        upper, v_now = ([], [])
+        for nth in range(n_dev_all - 1):
+            if nth % 2 == 0:
+                upper.append(lax.ppermute(upper[-1] if upper else my_tile, across, arrivals))
+            else:
+                oldest = lax.ppermute(v_now[-1] if v_now else my_tile, across, blocks_here)
+                v_now.append(oldest)
+        newest = jnp.stack([*upper[::-1], my_tile, *v_now])
+        b_next = lax.axis_index(across) - len(upper)
+        newest = newest[(jnp.arange(n_dev_all) - b_next) % n_dev_all]
+        return roots_open(newest, dim_i)
+
     attn_all, mixed_all, mlp_all, upstream_all = (
         lax.all_gather(attn_in, "seq", axis=0, tiled=True),
-        lax.all_gather(mixed_low, "seq", axis=0, tiled=True),
+        _place_boxes(mixed_low, "seq", 0),
         lax.all_gather(mlp_in, "seq", axis=0, tiled=True),
         lax.all_gather(upstream_low, "seq", axis=0, tiled=True),
     )

time: 1700 us -> 1680 us (0.988)
  waiting for transfers between devices: 1090 us -> 937 us
  starting transfers between devices: 31.8 us -> 134 us
  local copies, waits for them, and re-layouts: 137 us -> 159 us
    ppermute x0 -> x7, waiting for transfers between devices: none -> 177 us  [the longest x4 176 us: _place_boxes(): lax.ppermute(upper[-1] if upper else my_tile, across, arrivals)]
    all_gather x1, waiting for transfers between devices: 115 us -> 0.01 us  [on_device(): lax.all_gather(mlp_in, 'seq', axis=0, tiled=True)]
    unnamed x23 -> x22, waiting for transfers between devices: 89.3 us -> 4.69 us
    all_to_all x1, waiting for transfers between devices: 83.9 us -> 0.01 us  [on_device(): lax.all_to_all(split_columns(gate_grad, dp_count), 'seq', split_axis=2, c...]
    all_to_all x1, starting transfers between devices: 5.27 us -> 73.4 us  [on_device(): lax.all_to_all(split_columns(up_grad, dp_count), 'seq', split_axis=2, con...]
    all_gather x1 -> x0, waiting for transfers between devices: 57.7 us -> none  [on_device(): lax.all_gather(mixed_low, 'seq', axis=0, tiled=True)]
    ppermute x0 -> x7, starting transfers between devices: none -> 34.8 us  [the longest x4 27.7 us: _place_boxes(): lax.ppermute(upper[-1] if upper else my_tile, across, arrivals)]
    all_to_all x1, waiting for transfers between devices: 4.84 us -> 33.4 us  [on_device(): lax.all_to_all(split_columns(up_grad, dp_count), 'seq', split_axis=2, con...]
  transfers between devices with their start and end apart: 26 -> 32, of which waited for: 16 -> 16; matrix products, arithmetic and copies ran while one was open for 17% -> 19% of each run, Pallas kernels for 0% -> 0%
where the time goes in v1:
time: 1680 us; the launch traced here: 1670 us
  waiting for transfers between devices  937 us (56%)
  matrix products  200 us (12%)
  blocking collectives  176 us (10%)
  local copies, waits for them, and re-layouts  159 us (9%)
  starting transfers between devices  134 us (8%)
  other arithmetic  45.8 us (3%)
  between operations  17.1 us (1%)
    ppermute x4, waiting for transfers between devices, _place_boxes(): lax.ppermute(upper[-1] if upper else my_tile, across, arrivals)  176 us
    all_gather x1, waiting for transfers between devices, on_device(): lax.all_gather(gate_weight, ('dp', 'seq'), axis=0, tiled=True)  162 us
    all_gather x1, waiting for transfers between devices, on_device(): lax.all_gather(up_weight, ('dp', 'seq'), axis=0, tiled=True)  150 us
    all_gather x1, waiting for transfers between devices, on_device(): lax.all_gather(down_weight, ('dp', 'seq'), axis=1, tiled=True)  149 us
    unnamed x3, blocking collectives  90.3 us
    all_to_all x1, waiting for transfers between devices, on_device(): lax.all_to_all(split_columns(hidden_low, dp_count), 'seq', split_axis=2,...  88.4 us
    all_to_all x1, starting transfers between devices, on_device(): lax.all_to_all(split_columns(up_grad, dp_count), 'seq', split_axis=2, con...  73.4 us
    all_gather x1, waiting for transfers between devices, on_device(): lax.all_gather(q_weight, ('dp', 'seq'), axis=0, tiled=True)  63.2 us
  transfers between devices with their start and end apart: 32, of which 16 were waited for; matrix products, arithmetic and copies ran while one was open for 19% of the time, Pallas kernels for 0%

profile of v1, /device:TPU:0, one launch (start us, length us, event | category | flops | bytes accessed | tf_op | source)
XLA Modules:
  0.0 1669.7 jit_solution(11730609247259682478)
XLA Ops:
  11.5 42.2 %all-reduce.16 = (bf16[1536]{0:T(1024)(128)(2,1)S(1)}, bf16[256]{0:T(256)(128)(2,1)S(1)}, bf16[256]{0:T(256)(128)(2,1)S(1)}, bf16[1536]{0:T(1024)(128)(2,1)S(1)}, bf16[1536]{0:T(1024)(128)(2,1)S(1)}) all-reduce(bf16[1536]{0:T(1024)(128)(2,1)S(1)} %dynamic-update-slice, ...), channel_id=1, replica_groups=mesh['dp'=4,'seq'=8] {'dp','seq'}, use_global_device_ids=true, to_apply=%add | all-reduce | flops 5120 | bytes 20480
  55.1 43.7 %all_gather.59 = bf16[256,1536]{1,0:T(8,128)(2,1)S(1)} all-gather(bf16[8,1536]{1,0:T(8,128)(2,1)} %param.23), channel_id=1, replica_groups=mesh['dp'=4,'seq'=8] {'dp','seq'}, dimensions={0}, use_global_device_ids=true | all-gather | bytes 811008 | tf_op jit(solution)/shard_map/all_gather | solution.py:120
  101.7 41.6 %all_gather.62 = bf16[256,1536]{1,0:T(8,128)(2,1)S(1)} all-gather(bf16[8,1536]{1,0:T(8,128)(2,1)S(1)} %copy-done.53), channel_id=1, replica_groups=mesh['dp'=4,'seq'=8] {'dp','seq'}, dimensions={0}, use_global_device_ids=true | all-gather | bytes 811008 | tf_op jit(solution)/shard_map/all_gather | solution.py:118
  154.8 14.3 all-gather.13.cloned.1.call-done
  171.3 63.2 %all-gather.15.cloned.1.call-done = bf16[1536,1536]{1,0:T(8,128)(2,1)} async-done(((bf16[48,1536]{1,0:T(8,128)(2,1)}), bf16[1536,1536]{1,0:T(8,128)(2,1)}) %all-gather.15.cloned.1.call-update) | async-done | bytes 4718608 | tf_op jit(solution)/shard_map/all_gather | solution.py:116
  234.5 4.9 convolution_add_fusion.5
  257.2 42.1 %all-gather.17.cloned.1.call-done = bf16[1536,1536]{1,0:T(8,128)(2,1)} async-done(((bf16[48,1536]{1,0:T(8,128)(2,1)}), bf16[1536,1536]{1,0:T(8,128)(2,1)}) %all-gather.17.cloned.1.call-update) | async-done | bytes 4718608 | tf_op jit(solution)/shard_map/all_gather | solution.py:122
  299.3 4.0 multiply_reduce_fusion.4
  303.5 162.4 %all-gather.19.cloned.1.call-done = bf16[8960,1536]{1,0:T(8,128)(2,1)} async-done(((bf16[280,1536]{1,0:T(8,128)(2,1)}), bf16[8960,1536]{1,0:T(8,128)(2,1)}) %all-gather.19.cloned.1.call-update) | async-done | bytes 27525136 | tf_op jit(solution)/shard_map/all_gather | solution.py:168
  465.9 16.4 fusion.52
  482.3 150.2 %all-gather.21.cloned.1.call-done = bf16[8960,1536]{1,0:T(8,128)(2,1)} async-done(((bf16[280,1536]{1,0:T(8,128)(2,1)}), bf16[8960,1536]{1,0:T(8,128)(2,1)}) %all-gather.21.cloned.1.call-update) | async-done | bytes 27525136 | tf_op jit(solution)/shard_map/all_gather | solution.py:169
  632.4 17.2 %fusion.53 = f32[256,8960]{1,0:T(8,128)} fusion(bf16[256,1536]{1,0:T(8,128)(2,1)} %copy-done.26, bf16[8960,1536]{1,0:T(8,128)(2,1)} %all-gather.21.cloned.1.call-done), kind=kOutput, calls=%fused_computation.149 | convolution fusion | flops 7046430720 | bytes 37486592 | tf_op jit(solution)/shard_map/dot_general | solution.py:21
  649.6 149.4 %all-gather.23.cloned.1.call-done = bf16[1536,8960]{0,1:T(8,128)(2,1)} async-done(((bf16[1536,280]{0,1:T(8,128)(2,1)}), bf16[1536,8960]{0,1:T(8,128)(2,1)}) %all-gather.23.cloned.1.call-update) | async-done | bytes 27525136 | tf_op jit(solution)/shard_map/all_gather | solution.py:170
  799.0 20.0 %multiply_convert_fusion = (bf16[256,8960]{1,0:T(8,128)(2,1)S(1)}, bf16[256,8960]{1,0:T(8,128)(2,1)}, bf16[256,8960]{1,0:T(8,128)(2,1)}) fusion(f32[256,8960]{1,0:T(8,128)} %fusion.52, f32[256,8960]{1,0:T(8,128)} %fusion.53, bf16[256,1536]{1,0:T(8,128)(2,1)S(1)} %copy-done.25, bf16[1536,8960]{0,1:T(8,128)(2,1)} %all-gather.23.cloned.1.call-done), kind=kOutput, calls=%fused_computation.1 | convolution fusion | flops 7083130880 | bytes 60424192 | tf_op jit(solution)/shard_map/dot_general | solution.py:27
  819.1 16.4 fusion.54
  835.5 14.8 multiply_reduce_fusion
  855.9 4.4 fusion
  867.0 4.4 fusion.3
  877.5 4.0 fusion.10
  882.8 4.9 fusion.12
  887.7 2.7 copy.182
  890.4 3.0 pad_maximum_fusion.1
  903.5 3.5 all-to-all-start
  909.2 24.1 %all-to-all-done = bf16[256,4,384]{0,1,2:T(4,128)(2,1)S(1)} async-done(((bf16[256,4,384]{0,1,2:T(4,128)(2,1)}), bf16[256,4,384]{0,1,2:T(4,128)(2,1)S(1)}, u32[]{:S(2)}, u32[]{:S(2)}) %all-to-all-start) | async-done | bytes 786464 | tf_op jit(solution)/shard_map/all_to_all | solution.py:319
  933.3 3.6 all-to-all-start.3
  941.5 23.7 %all-to-all-done.3 = bf16[256,4,384]{0,1,2:T(4,128)(2,1)S(1)} async-done(((bf16[256,4,384]{0,1,2:T(4,128)(2,1)}), bf16[256,4,384]{0,1,2:T(4,128)(2,1)S(1)}, u32[]{:S(2)}, u32[]{:S(2)}) %all-to-all-start.3) | async-done | bytes 786464 | tf_op jit(solution)/shard_map/all_to_all | solution.py:316
  965.2 3.4 all-to-all-start.1
  970.6 4.7 all-to-all-done.1
  975.3 4.2 all-to-all-start.2
  979.5 6.6 copy.198
  986.1 18.3 %copy.199 = bf16[256,4,2240]{0,1,2:T(4,128)(2,1)} copy(bf16[256,4,2240]{0,2,1:T(8,128)(2,1)} %bitcast.331) | data formatting | bytes 9175040 | tf_op jit(solution)/shard_map/reshape | solution.py:32
  1004.4 5.2 all-to-all-start.4
  1011.3 146.0 %collective-permute-done = bf16[256,1536]{1,0:T(8,128)(2,1)S(1)} collective-permute-done((bf16[256,1536]{1,0:T(8,128)(2,1)S(1)}, bf16[256,1536]{1,0:T(8,128)(2,1)S(1)}, u32[]{:S(2)}, u32[]{:S(2)}) %collective-permute-start) | collective-permute-done | bytes 786464 | tf_op jit(solution)/shard_map/ppermute | solution.py:204
  1158.2 3.5 collective-permute-start.4
  1161.7 19.7 %collective-permute-done.1 = bf16[256,1536]{1,0:T(8,128)(2,1)S(1)} collective-permute-done((bf16[256,1536]{1,0:T(8,128)(2,1)S(1)}, bf16[256,1536]{1,0:T(8,128)(2,1)S(1)}, u32[]{:S(2)}, u32[]{:S(2)}) %collective-permute-start.1) | collective-permute-done | bytes 786464 | tf_op jit(solution)/shard_map/ppermute | solution.py:204
  1182.3 3.5 collective-permute-start.5
  1185.8 9.9 collective-permute-done.2
  1195.7 27.3 %collective-permute-start.3 = (bf16[256,1536]{1,0:T(8,128)(2,1)}, bf16[256,1536]{1,0:T(8,128)(2,1)}, u32[]{:S(2)}, u32[]{:S(2)}) collective-permute-start(bf16[256,1536]{1,0:T(8,128)(2,1)} %collective-permute-done.2), channel_id=1, source_target_pairs={{0,1},{1,2},{2,3},{3,4},{4,5},{5,6},{6,7},{7,0},{8,9},{9,10},{10,1... | collective-permute-start | bytes 2359304 | tf_op jit(solution)/shard_map/ppermute | solution.py:204
  1236.2 6.6 copy.202
  1242.8 18.3 %copy.203 = bf16[256,4,2240]{0,1,2:T(4,128)(2,1)} copy(bf16[256,4,2240]{0,2,1:T(8,128)(2,1)} %bitcast.332) | data formatting | bytes 9175040 | tf_op jit(solution)/shard_map/reshape | solution.py:32
  1261.3 5.0 convolution_convert_fusion.5
  1266.3 73.4 %all-to-all-start.5 = ((bf16[256,4,2240]{0,1,2:T(4,128)(2,1)}), bf16[256,4,2240]{0,1,2:T(4,128)(2,1)}, u32[]{:S(2)}, u32[]{:S(2)}) async-start(bf16[256,4,2240]{0,1,2:T(4,128)(2,1)} %copy.203), calls=%async_computation.9 | async-start | bytes 9175040 | tf_op jit(solution)/shard_map/all_to_all | solution.py:232
  1344.3 6.4 gather_fusion
  1350.9 5.1 convolution_convert_fusion.4
  1357.1 4.6 convolution_convert_fusion.7
  1361.7 4.6 convolution_convert_fusion.6
  1366.3 2.9 copy.200
  1369.2 2.7 copy.253
  1372.0 12.1 convolution_convert_fusion.2
  1384.1 6.6 copy.206
  1390.6 18.2 %copy.207 = bf16[256,4,2240]{0,1,2:T(4,128)(2,1)} copy(bf16[256,4,2240]{0,2,1:T(8,128)(2,1)} %bitcast.336) | data formatting | bytes 9175040 | tf_op jit(solution)/shard_map/reshape | solution.py:32
  1408.8 33.4 %all-to-all-done.5 = bf16[256,4,2240]{0,1,2:T(4,128)(2,1)} async-done(((bf16[256,4,2240]{0,1,2:T(4,128)(2,1)}), bf16[256,4,2240]{0,1,2:T(4,128)(2,1)}, u32[]{:S(2)}, u32[]{:S(2)}) %all-to-all-start.5) | async-done | bytes 4587552 | tf_op jit(solution)/shard_map/all_to_all | solution.py:232
  1442.2 4.8 all-to-all-start.6
  1447.0 3.0 copy.204
  1452.0 8.8 convolution_convert_fusion.1
  1461.0 88.4 %all-to-all-done.6 = bf16[256,4,2240]{0,1,2:T(4,128)(2,1)} async-done(((bf16[256,4,2240]{0,1,2:T(4,128)(2,1)}), bf16[256,4,2240]{0,1,2:T(4,128)(2,1)}, u32[]{:S(2)}, u32[]{:S(2)}) %all-to-all-start.6) | async-done | bytes 4587552 | tf_op jit(solution)/shard_map/all_to_all | solution.py:226
  1549.3 2.9 copy.208
  1552.2 2.7 copy.255
  1555.0 12.0 convolution_convert_fusion
  1569.8 5.0 fusion.30
  1574.9 15.0 fusion.19
  1598.9 38.4 %all-reduce.15 = (f32[1536]{0:T(1024)S(1)}, f32[1536]{0:T(1024)S(1)}) all-reduce(f32[1536]{0:T(1024)S(1)} %get-tuple-element.16, f32[1536]{0:T(1024)S(1)} %copy-done.56), channel_id=4, replica_groups=mesh['dp'=4,'seq'=8] {'dp','seq'}, use_global_device_ids=true, to_apply=%region_13.14.clone | all-reduce | flops 3072 | bytes 24576
  1638.5 3.0 multiply_add_fusion
  1642.7 9.7 all-reduce.17
  (347 shorter events, 126.0 us)
Async XLA Ops:
  7.2 94.5 %copy-start.53 = (bf16[8,1536]{1,0:T(8,128)(2,1)S(1)}, bf16[8,1536]{1,0:T(8,128)(2,1)}, u32[]{:S(2)}) copy-start(bf16[8,1536]{1,0:T(8,128)(2,1)} %param.21) | copy-start | bytes 73732
  7.2 144.3 %all-gather.11.cloned.1.call-start = ((), (), s32[]{:S(2)}) async-start(), calls=%async_computation.14 | async-start | bytes 1179648 | tf_op jit(solution)/shard_map/all_gather | solution.py:143
  53.7 45.1 %copy-start.51 = (f32[1536]{0:T(1024)}, f32[1536]{0:T(1024)S(1)}, u32[]{:S(2)}) copy-start(f32[1536]{0:T(1024)S(1)} %convert_element_type.207) | copy-start | bytes 18436
  55.1 43.7 %copy-start.54 = (f32[256]{0:T(256)}, f32[256]{0:T(256)S(1)}, u32[]{:S(2)}) copy-start(f32[256]{0:T(256)S(1)} %rsqrt_bitcast_fusion) | copy-start | bytes 3076
  100.5 134.0 %copy-start.8 = (bf16[256,1536]{1,0:T(8,128)(2,1)}, bf16[256,1536]{1,0:T(8,128)(2,1)S(1)}, u32[]{:S(2)}) copy-start(bf16[256,1536]{1,0:T(8,128)(2,1)S(1)} %multiply_convert_fusion.4) | copy-start | bytes 2359300
  101.6 67.4 %all-gather.13.cloned.1.call-start = ((), (), s32[]{:S(2)}) async-start(), calls=%async_computation.15 | async-start | bytes 1179648 | tf_op jit(solution)/shard_map/all_gather | solution.py:142
  146.0 96.6 %copy-start.34 = (f32[128,128]{0,1:T(8,128)}, f32[128,128]{0,1:T(8,128)S(1)}, u32[]{:S(2)}) copy-start(f32[128,128]{0,1:T(8,128)S(1)} %get-tuple-element.51) | copy-start | bytes 196612
  146.0 96.6 %copy-start.36 = (f32[128,128]{0,1:T(8,128)}, f32[128,128]{0,1:T(8,128)S(1)}, u32[]{:S(2)}) copy-start(f32[128,128]{0,1:T(8,128)S(1)} %get-tuple-element.52) | copy-start | bytes 196612
  146.8 87.7 %all-gather.15.cloned.1.call-start = ((), (), s32[]{:S(2)}) async-start(), calls=%async_computation.16 | async-start | bytes 4866048 | tf_op jit(solution)/shard_map/all_gather | solution.py:116
  147.5 151.7 %all-gather.17.cloned.1.call-start = ((), (), s32[]{:S(2)}) async-start(), calls=%async_computation.17 | async-start | bytes 4866048 | tf_op jit(solution)/shard_map/all_gather | solution.py:122
  148.1 317.8 %all-gather.19.cloned.1.call-start = ((), (), s32[]{:S(2)}) async-start(), calls=%async_computation.18 | async-start | bytes 28385280 | tf_op jit(solution)/shard_map/all_gather | solution.py:168
  148.7 483.7 %all-gather.21.cloned.1.call-start = ((), (), s32[]{:S(2)}) async-start(), calls=%async_computation.19 | async-start | bytes 28385280 | tf_op jit(solution)/shard_map/all_gather | solution.py:169
  149.3 649.7 %all-gather.23.cloned.1.call-start = ((), (), s32[]{:S(2)}) async-start(), calls=%async_computation.20 | async-start | bytes 28385280 | tf_op jit(solution)/shard_map/all_gather | solution.py:170
  150.0 787.2 %reduce-scatter.14.cloned.1.call-start = ((), (), s32[]{:S(2)}) async-start(), calls=%async_computation.21 | async-start | bytes 2359296 | tf_op jit(solution)/shard_map/reduce_scatter | solution.py:293
  150.2 700.1 %copy-start.57 = (pred[256]{0:T(512)(128)(4,1)}, pred[256]{0:T(512)(128)(4,1)S(1)}, u32[]{:S(2)}) copy-start(pred[256]{0:T(512)(128)(4,1)S(1)} %compare_bitcast_fusion) | copy-start | bytes 772
  255.0 44.3 %copy-start.6 = (bf16[2,128,1536]{2,1,0:T(8,128)(2,1)S(1)}, bf16[2,128,1536]{2,1,0:T(8,128)(2,1)}, u32[]{:S(2)}) copy-start(bf16[2,128,1536]{2,1,0:T(8,128)(2,1)} %param.15) | copy-start | bytes 2359300
  255.0 44.3 %copy-start.42 = (bf16[128,1536]{1,0:T(8,128)(2,1)S(1)}, bf16[128,1536]{1,0:T(8,128)(2,1)}, u32[]{:S(2)}) copy-start(bf16[128,1536]{1,0:T(8,128)(2,1)} %copy.160) | copy-start | bytes 1179652
  256.3 43.0 %copy-start.40 = (bf16[2,128,6,128]{3,1,2,0:T(8,128)(2,1)}, bf16[2,128,6,128]{3,1,2,0:T(8,128)(2,1)S(1)}, u32[]{:S(2)}) copy-start(bf16[2,128,6,128]{3,1,2,0:T(8,128)(2,1)S(1)} %fusion.28) | copy-start | bytes 1179652
  303.3 547.1 %copy-start.12 = (f32[256,1536]{1,0:T(8,128)}, f32[256,1536]{1,0:T(8,128)S(1)}, u32[]{:S(2)}) copy-start(f32[256,1536]{1,0:T(8,128)S(1)} %get-tuple-element.58) | copy-start | bytes 4718596
  303.5 162.4 %copy-start.26 = (bf16[256,1536]{1,0:T(8,128)(2,1)}, bf16[256,1536]{1,0:T(8,128)(2,1)S(1)}, u32[]{:S(2)}) copy-start(bf16[256,1536]{1,0:T(8,128)(2,1)S(1)} %multiply_convert_fusion.3) | copy-start | bytes 2359300
  482.3 316.8 %copy-start.25 = (bf16[256,1536]{1,0:T(8,128)(2,1)S(1)}, bf16[256,1536]{1,0:T(8,128)(2,1)}, u32[]{:S(2)}) copy-start(bf16[256,1536]{1,0:T(8,128)(2,1)} %fusion.24) | copy-start | bytes 2359300
  819.1 16.4 copy-start.16
  835.5 16.6 slice-start.8
  835.5 14.9 copy-start.22
  835.5 16.6 slice-start.9
  852.0 8.3 slice-start
  863.3 8.1 slice-start.2
  877.4 91.2 %reduce-scatter.16.cloned.1.call-start = ((), (), s32[]{:S(2)}) async-start(), calls=%async_computation.22 | async-start | bytes 2359296 | tf_op jit(solution)/shard_map/reduce_scatter | solution.py:294
  893.5 367.8 %all-gather.25.cloned.1.call-start = ((), (), s32[]{:S(2)}) async-start(), calls=%async_computation.23 | async-start | bytes 7077888 | tf_op jit(solution)/shard_map/all_gather | solution.py:214
  894.1 477.9 %all-gather.27.cloned.1.call-start = ((), (), s32[]{:S(2)}) async-start(), calls=%async_computation.26 | async-start | bytes 7077888 | tf_op jit(solution)/shard_map/all_gather | solution.py:216
  899.5 8.2 copy-start.24
  903.5 29.8 %all-to-all-start = ((bf16[256,4,384]{0,1,2:T(4,128)(2,1)}), bf16[256,4,384]{0,1,2:T(4,128)(2,1)S(1)}, u32[]{:S(2)}, u32[]{:S(2)}) async-start(bf16[256,4,384]{0,1,2:T(4,128)(2,1)} %copy.184), calls=%async_computation.2 | async-start | bytes 1572864 | tf_op jit(solution)/shard_map/all_to_all | solution.py:319
  907.1 647.9 %all-gather.29.cloned.1.call-start = ((), (), s32[]{:S(2)}) async-start(), calls=%async_computation.27 | async-start | bytes 7077888 | tf_op jit(solution)/shard_map/all_gather | solution.py:217
  933.3 31.9 %all-to-all-start.3 = ((bf16[256,4,384]{0,1,2:T(4,128)(2,1)}), bf16[256,4,384]{0,1,2:T(4,128)(2,1)S(1)}, u32[]{:S(2)}, u32[]{:S(2)}) async-start(bf16[256,4,384]{0,1,2:T(4,128)(2,1)} %copy.193), calls=%async_computation.6 | async-start | bytes 1572864 | tf_op jit(solution)/shard_map/all_to_all | solution.py:316
  938.8 47.3 %copy-start.30 = (f32[2,128,2,128]{1,0,3,2:T(2,128)}, f32[2,128,2,128]{1,0,3,2:T(2,128)S(1)}, u32[]{:S(2)}) copy-start(f32[2,128,2,128]{1,0,3,2:T(2,128)S(1)} %pad_maximum_fusion.5) | copy-start | bytes 786436
  965.2 10.1 all-to-all-start.1
  975.3 10.8 copy-start.45
  975.3 29.1 %all-to-all-start.2 = ((bf16[256,4,64]{0,1,2:T(4,128)(2,1)}), bf16[256,4,64]{0,1,2:T(4,128)(2,1)}, u32[]{:S(2)}, u32[]{:S(2)}) async-start(bf16[256,4,64]{0,1,2:T(4,128)(2,1)} %copy.191), calls=%async_computation.5 | async-start | bytes 262144 | tf_op jit(solution)/shard_map/all_to_all | solution.py:325
  1004.4 218.6 %copy-start.39 = (bf16[2,128,6,128]{3,1,2,0:T(8,128)(2,1)S(1)}, bf16[2,128,6,128]{3,1,2,0:T(8,128)(2,1)}, u32[]{:S(2)}) copy-start(bf16[2,128,6,128]{3,1,2,0:T(8,128)(2,1)} %copy-done.38) | copy-start | bytes 1179652
  1004.4 219.6 %copy-start.41 = (bf16[2,128,6,128]{3,1,2,0:T(8,128)(2,1)S(1)}, bf16[2,128,6,128]{3,1,2,0:T(8,128)(2,1)}, u32[]{:S(2)}) copy-start(bf16[2,128,6,128]{3,1,2,0:T(8,128)(2,1)} %copy-done.40) | copy-start | bytes 1179652
  1004.4 261.9 %all-to-all-start.4 = ((bf16[256,4,2240]{0,1,2:T(4,128)(2,1)}), bf16[256,4,2240]{0,1,2:T(4,128)(2,1)}, u32[]{:S(2)}, u32[]{:S(2)}) async-start(bf16[256,4,2240]{0,1,2:T(4,128)(2,1)} %copy.199), calls=%async_computation.8 | async-start | bytes 9175040 | tf_op jit(solution)/shard_map/all_to_all | solution.py:229
  1009.6 581.1 %reduce-scatter.18.cloned.1.call-start = ((), (), s32[]{:S(2)}) async-start(), calls=%async_computation.24 | async-start | bytes 737280 | tf_op jit(solution)/shard_map/reduce_scatter | solution.py:337
  1010.9 146.4 %collective-permute-start = (bf16[256,1536]{1,0:T(8,128)(2,1)S(1)}, bf16[256,1536]{1,0:T(8,128)(2,1)S(1)}, u32[]{:S(2)}, u32[]{:S(2)}) collective-permute-start(bf16[256,1536]{1,0:T(8,128)(2,1)S(1)} %pad_maximum_fusion.3), channel_id=1, source_target_pairs={{0,1},{1,2},{2,3},{3,4},{4,5},{5,6},{6,7},{7,0},{8,9},{9,10},{10,1... | collective-permute-start | bytes 2359304 | tf_op jit(solution)/shard_map/ppermute | solution.py:204
  1158.2 23.2 %collective-permute-start.1 = (bf16[256,1536]{1,0:T(8,128)(2,1)S(1)}, bf16[256,1536]{1,0:T(8,128)(2,1)S(1)}, u32[]{:S(2)}, u32[]{:S(2)}) collective-permute-start(bf16[256,1536]{1,0:T(8,128)(2,1)S(1)} %collective-permute-done), channel_id=1, source_target_pairs={{0,1},{1,2},{2,3},{3,4},{4,5},{5,6},{6,7},{7,0},{8,9},{9,10},{10,1... | collective-permute-start | bytes 2359304 | tf_op jit(solution)/shard_map/ppermute | solution.py:204
  1158.2 24.1 %collective-permute-start.4 = (bf16[256,1536]{1,0:T(8,128)(2,1)S(1)}, bf16[256,1536]{1,0:T(8,128)(2,1)}, u32[]{:S(2)}, u32[]{:S(2)}) collective-permute-start(bf16[256,1536]{1,0:T(8,128)(2,1)S(1)} %pad_maximum_fusion.3), channel_id=1, source_target_pairs={{1,0},{2,1},{3,2},{4,3},{5,4},{6,5},{7,6},{0,7},{9,8},{10,9},{11,1... | collective-permute-start | bytes 2359304 | tf_op jit(solution)/shard_map/ppermute | solution.py:206
  1182.3 13.4 collective-permute-start.2
  1182.3 43.6 %collective-permute-start.5 = (bf16[256,1536]{1,0:T(8,128)(2,1)}, bf16[256,1536]{1,0:T(8,128)(2,1)}, u32[]{:S(2)}, u32[]{:S(2)}) collective-permute-start(bf16[256,1536]{1,0:T(8,128)(2,1)} %collective-permute-done.4), channel_id=1, source_target_pairs={{1,0},{2,1},{3,2},{4,3},{5,4},{6,5},{7,6},{0,7},{9,8},{10,9},{11,1... | collective-permute-start | bytes 2359304 | tf_op jit(solution)/shard_map/ppermute | solution.py:206
  1195.7 30.4 %collective-permute-start.3 = (bf16[256,1536]{1,0:T(8,128)(2,1)}, bf16[256,1536]{1,0:T(8,128)(2,1)}, u32[]{:S(2)}, u32[]{:S(2)}) collective-permute-start(bf16[256,1536]{1,0:T(8,128)(2,1)} %collective-permute-done.2), channel_id=1, source_target_pairs={{0,1},{1,2},{2,3},{3,4},{4,5},{5,6},{6,7},{7,0},{8,9},{9,10},{10,1... | collective-permute-start | bytes 2359304 | tf_op jit(solution)/shard_map/ppermute | solution.py:204
  1224.0 9.2 copy-start.43
  1224.9 8.3 copy-start.44
  1225.8 116.4 %collective-permute-start.6 = (bf16[256,1536]{1,0:T(8,128)(2,1)}, bf16[256,1536]{1,0:T(8,128)(2,1)}, u32[]{:S(2)}, u32[]{:S(2)}) collective-permute-start(bf16[256,1536]{1,0:T(8,128)(2,1)} %collective-permute-done.5), channel_id=1, source_target_pairs={{1,0},{2,1},{3,2},{4,3},{5,4},{6,5},{7,6},{0,7},{9,8},{10,9},{11,1... | collective-permute-start | bytes 2359304 | tf_op jit(solution)/shard_map/ppermute | solution.py:206
  1266.3 175.9 %all-to-all-start.5 = ((bf16[256,4,2240]{0,1,2:T(4,128)(2,1)}), bf16[256,4,2240]{0,1,2:T(4,128)(2,1)}, u32[]{:S(2)}, u32[]{:S(2)}) async-start(bf16[256,4,2240]{0,1,2:T(4,128)(2,1)} %copy.203), calls=%async_computation.9 | async-start | bytes 9175040 | tf_op jit(solution)/shard_map/all_to_all | solution.py:232
  1339.6 252.7 %reduce-scatter.20.cloned.1.call-start = ((), (), s32[]{:S(2)}) async-start(), calls=%async_computation.25 | async-start | bytes 737280 | tf_op jit(solution)/shard_map/reduce_scatter | solution.py:355
  1356.1 297.5 %all-reduce.21.cloned.1.call-start = ((), (), s32[]{:S(2)}) async-start(), calls=%async_computation.31 | async-start | bytes 393216
  1366.3 288.7 %reduce-scatter.22.cloned.1.call-start = ((), (), s32[]{:S(2)}) async-start(), calls=%async_computation.28 | async-start | bytes 4300800
  1442.2 107.2 %all-to-all-start.6 = ((bf16[256,4,2240]{0,1,2:T(4,128)(2,1)}), bf16[256,4,2240]{0,1,2:T(4,128)(2,1)}, u32[]{:S(2)}, u32[]{:S(2)}) async-start(bf16[256,4,2240]{0,1,2:T(4,128)(2,1)} %copy.207), calls=%async_computation.10 | async-start | bytes 9175040 | tf_op jit(solution)/shard_map/all_to_all | solution.py:226
  1446.9 210.6 %reduce-scatter.24.cloned.1.call-start = ((), (), s32[]{:S(2)}) async-start(), calls=%async_computation.29 | async-start | bytes 4300800
  1460.8 199.4 %reduce-scatter.26.cloned.1.call-start = ((), (), s32[]{:S(2)}) async-start(), calls=%async_computation.30 | async-start | bytes 4300800
  1555.0 12.9 copy-start.60
  1574.9 19.2 %copy-start.31 = (f32[2,128,2,128]{1,0,3,2:T(2,128)S(1)}, f32[2,128,2,128]{1,0,3,2:T(2,128)}, u32[]{:S(2)}) copy-start(f32[2,128,2,128]{1,0,3,2:T(2,128)} %copy-done.30) | copy-start | bytes 786436
  1574.9 20.4 %copy-start.10 = (bf16[256,1536]{1,0:T(8,128)(2,1)S(1)}, bf16[256,1536]{1,0:T(8,128)(2,1)}, u32[]{:S(2)}) copy-start(bf16[256,1536]{1,0:T(8,128)(2,1)} %copy-done.9) | copy-start | bytes 2359300
  1597.1 41.4 %copy-start.11 = (f32[256,1536]{1,0:T(8,128)S(1)}, f32[256,1536]{1,0:T(8,128)}, u32[]{:S(2)}) copy-start(f32[256,1536]{1,0:T(8,128)} %get-tuple-element.31) | copy-start | bytes 4718596
  1597.1 44.3 %copy-start.47 = (bf16[256,4,64]{0,1,2:T(4,128)(2,1)S(1)}, bf16[256,4,64]{0,1,2:T(4,128)(2,1)}, u32[]{:S(2)}) copy-start(bf16[256,4,64]{0,1,2:T(4,128)(2,1)} %copy-done.45) | copy-start | bytes 393220
  1597.1 45.6 %copy-start.61 = (bf16[192]{0:T(256)(128)(2,1)S(1)}, bf16[192]{0:T(256)(128)(2,1)}, u32[]{:S(2)}) copy-start(bf16[192]{0:T(256)(128)(2,1)} %convert_element_type.242) | copy-start | bytes 1156
  (40 other events, 150.8 us)
Sparse Core Ops, SparseCore 0:
  101.7 21.1 all-gather.10
  146.9 22.0 all-gather.12
  172.1 62.3 all-gather.14
  237.3 61.9 all-gather.16
  302.2 163.6 all-gather.18
  468.8 163.5 all-gather.20
  635.4 163.5 all-gather.22
  877.5 34.3 reduce-scatter.13
  914.2 40.8 reduce-scatter.15
  956.6 97.0 all-gather.24
  1055.9 159.6 all-gather.26
  1217.1 74.5 all-gather.28
  1295.1 66.5 reduce-scatter.17
  1364.4 25.4 reduce-scatter.19
  1392.6 42.6 all-reduce.20
  1438.3 46.3 reduce-scatter.21
  1487.5 46.3 reduce-scatter.23
  1567.1 45.9 reduce-scatter.25
